TPU v7x, 128 devices: a whole 4x4x4 slice. The times are simulated.
128 devices in a mesh: scan: 16 (over z, y), row: 8 (over x, core).
Axes of the slice: x: 4, y: 4, z: 4, core: 2. Of those that a mesh axis runs over, the one named last changes fastest.
Arguments:
- raw_planes: float32 [32, 6, 128, 1024], P('scan', None, 'row'), may hold values from 0 to 4
- shear_tiles: int32 [32], P('scan'), may hold values from 0 to 5, as said below
- axial_kernel: float32 [64], replicated, may hold values from 0.05 to 1
- column_kernel: float32 [31], replicated, may hold values from 0.05 to 1
- row_kernel: float32 [31], replicated, may hold values from 0.05 to 1
Outputs:
- estimate: float32 [32, 16, 128, 1024], P(None, 'scan', 'row')
Inputs may be any that keep to these rules, and one draw needn't show every extreme that they name: `shear_tiles`: plane p has a shear within one tile of p * 5 // 31; the first plane has 0 and the last 5.
All inputs are finite; a program needn't handle non-finite values.
Results may differ from a plain program's by a relative error of at most 0.0003.
Values sent between devices are 32-bit elements; how exact they have to be, the bound alone decides.
A program may use at most 128 MiB of HBM per device.

v0:
```python
import jax
import jax.numpy as jnp
from jax import lax
from jax.sharding import PartitionSpec as P

TILES_DEV = 1
ITERS = 2
background_level = 0.5


def normalized(kernel):
    return kernel / jnp.sum(kernel)


def band_matrix(kernel, extent):
    length = kernel.shape[0]
    centre = length // 2
    indices = jnp.arange(extent, dtype=jnp.int32)
    offset = indices[None, :] - indices[:, None] + centre
    inside = (offset >= 0) & (offset < length)
    return jnp.where(inside, kernel[jnp.clip(offset, 0, length - 1)], 0.0)


def shifted_sum(volume, kernel, centre, axis):
    length = kernel.shape[0]
    extent = volume.shape[axis]
    widths = [(0, 0)] * volume.ndim
    widths[axis] = (centre, length - 1 - centre)
    padded = jnp.pad(volume, widths)
    summed = jnp.zeros_like(volume)
    for tap in range(length):
        summed = summed + kernel[tap] * lax.slice_in_dim(padded, tap, tap + extent, axis=axis)
    return summed


def spread_planes(tiles_in, shear_tiles, total):

    def place_plane(one_plane, offset):
        empty_slab = jnp.zeros((total,) + one_plane.shape[1:], one_plane.dtype)
        anchor = jnp.zeros((), jnp.int32)
        return lax.dynamic_update_slice(empty_slab, one_plane, (offset, anchor, anchor))

    return jax.vmap(place_plane)(tiles_in, shear_tiles)


def axial_apply(matrix, volume):
    flattened = volume.reshape(volume.shape[0], -1)
    result = jnp.dot(matrix, flattened, precision=lax.Precision.HIGHEST)
    return result.reshape(volume.shape)


def rows_layout(volume):
    result = lax.all_to_all(
        lax.all_to_all(volume, "scan", split_axis=0, concat_axis=1, tiled=True),
        "row",
        split_axis=3,
        concat_axis=2,
        tiled=True,
    )
    return result


def pencil_layout(volume):
    result = lax.all_to_all(
        lax.all_to_all(volume, "scan", split_axis=1, concat_axis=0, tiled=True),
        "row",
        split_axis=2,
        concat_axis=3,
        tiled=True,
    )
    return result


def shards(raw_planes, shear_tiles, axial_kernel, column_kernel, row_kernel):
    scan_count = lax.axis_size("scan")
    out_count = TILES_DEV * scan_count
    axial = normalized(axial_kernel)
    across = normalized(column_kernel)
    down = normalized(row_kernel)
    lateral_len = across.shape[0]
    lateral_centre = lateral_len // 2
    back_centre = lateral_len - 1 - lateral_centre
    spread = spread_planes(raw_planes, shear_tiles, out_count)
    data_pencils = lax.all_to_all(spread, "scan", split_axis=1, concat_axis=0, tiled=True)
    data_rows = rows_layout(data_pencils)
    row_shape = data_rows.shape
    data_flat = data_rows.reshape(row_shape[0], row_shape[1] * row_shape[2], row_shape[3])
    axial_band = band_matrix(axial, data_pencils.shape[0])
    estimate = data_pencils + 1.0
    for iteration in range(ITERS):
        blurred = axial_apply(axial_band, estimate)
        blurred = shifted_sum(blurred, across, lateral_centre, 3)
        blurred_rows = rows_layout(blurred)
        flattened = blurred_rows.reshape(data_flat.shape)
        flattened = shifted_sum(flattened, down, lateral_centre, 1)
        quotient = data_flat / (flattened + background_level)
        quotient = shifted_sum(quotient, down[::-1], back_centre, 1)
        correction = pencil_layout(quotient.reshape(row_shape))
        correction = shifted_sum(correction, across[::-1], back_centre, 3)
        correction = axial_apply(axial_band.T, correction)
        estimate = estimate * correction
    return estimate


def solution(mesh):
    return jax.shard_map(
        shards,
        mesh=mesh,
        in_specs=(P("scan", None, "row", None), P("scan"), P(), P(), P()),
        out_specs=P(None, "scan", "row", None),
        check_vma=False,
    )
```

profile of v0, /device:TPU:1, one launch (start us, length us, event | category | flops | bytes accessed | tf_op | source)
XLA Modules:
  0.0 926.5 jit_solution(2786880016588994488)
XLA Ops:
  3.2 17.7 %while.1 = (s32[]{:T(128)}, f32[2,16,16,1024]{3,2,0,1:T(8,128)}, s32[2,4]{1,0:T(2,128)S(1)}, f32[2,6,16,1024]{3,2,1,0:T(8,128)S(1)}, s32[]{:T(128)}, /*index=5*/s32[4]{0:T(128)S(1)}) while((s32[]{:T(128)}, f32[2,16,16,1024]{3,2,0,1:T(8,128)}, s32[2,4]{1,0:T(2,128)S(1)}, f32[2,6,16,1024]{3,2,1,0:T(8,128)S(1)}, s32[]{:T(128)}, ...), condition=%wide.while_cond, body=%wide.while_body.sunk | while | flops 98333 | bytes 1968306 | solution.py:41
  20.8 8.8 all-to-all-start
  40.5 19.7 %all-to-all-done = f32[2,16,16,1024]{3,2,0,1:T(8,128)} async-done(((f32[2,16,16,1024]{3,2,0,1:T(8,128)}), f32[2,16,16,1024]{3,2,0,1:T(8,128)}, u32[]{:S(2)}, u32[]{:S(2)}) %all-to-all-start) | async-done | bytes 2097184 | tf_op jit(solution)/shard_map/all_to_all | solution.py:84
  66.4 36.0 %fusion.53 = f32[32,1,16,1024]{3,2,1,0:T(8,128)S(1)} fusion(f32[32,1,16,1024]{3,2,1,0:T(8,128)S(1)} %bitcast.299, f32[]{:T(128)} %bitcast.50, f32[]{:T(128)} %bitcast.49, f32[]{:T(128)} %bitcast.48, f32[]{:T(128)} %bitcast.47, f32[]{:T(128)} %bitcast.46, f32[]{:T(128)} %bitcast.45, f32[]{:T(128)} %bitcast.44, f32[]{:T(128)} %bitcast.43, f32[]{:T(128)} %bitcast.42, ...), kind=kLoop, calls=%fused_computation.179 | loop fusion | flops 31981568 | bytes 4194428 | tf_op jit(solution)/shard_map/add | solution.py:32
  102.4 31.3 %all_to_all.189 = f32[32,1,16,1024]{3,2,1,0:T(8,128)} all-to-all(f32[32,1,16,1024]{3,2,1,0:T(8,128)S(1)} %fusion.53), channel_id=1, replica_groups=mesh['scan'=16,'row'=8] {'scan'}, dimensions={0} | all-to-all | bytes 4194304 | tf_op jit(solution)/shard_map/all_to_all | solution.py:54
  137.7 21.4 %copy.97 = f32[2,16,16,1024]{2,0,1,3:T(2,128)} copy(f32[2,16,16,1024]{3,2,0,1:T(8,128)} %bitcast.293) | data formatting | bytes 4194304 | tf_op jit(solution)/shard_map/all_to_all | solution.py:54
  159.1 24.7 %reshape.188 = f32[8,1,65536]{2,1,0:T(1,128)} reshape(f32[1024,16,2,16]{3,2,1,0:T(2,128)} %bitcast.282) | data formatting | bytes 4194304
  190.4 13.6 %copy.92 = f32[16,2,1,16,1024]{3,0,1,4,2:T(8,128)} copy(f32[16,2,1,16,1024]{4,3,1,0,2:T(8,128)S(1)} %bitcast.292) | data formatting | bytes 4194304 | tf_op jit(solution)/shard_map/all_to_all | solution.py:54
  204.0 11.6 %bitcast_bitcast_fusion = f32[1024,2,16,16]{3,2,1,0:T(8,128)} fusion(f32[16,2,1,16,1024]{3,0,1,4,2:T(8,128)} %copy.92), kind=kLoop, calls=%fused_computation.512 | loop fusion | bytes 4194304
  215.6 11.6 %reshape.186 = f32[8,1,65536]{2,1,0:T(1,128)} reshape(f32[1024,2,16,16]{3,2,1,0:T(8,128)} %bitcast_bitcast_fusion) | data formatting | bytes 4194304
  244.2 28.4 %reshape.189 = f32[1024,16,2,16]{3,2,1,0:T(2,128)} reshape(f32[8,65536]{1,0:T(8,128)S(1)} %reduce.3) | data formatting | bytes 4194304
  272.6 21.8 %copy.130 = f32[2,16,16,8,128]{4,2,3,1,0:T(8,128)} copy(f32[2,16,16,8,128]{2,0,1,4,3:T(2,128)} %bitcast.283) | data formatting | bytes 4194304 | tf_op jit(solution)/shard_map/all_to_all | solution.py:53
  301.7 11.3 %reshape.187 = f32[1024,2,16,16]{3,2,1,0:T(8,128)} reshape(f32[8,65536]{1,0:T(8,128)S(1)} %reduce.2) | data formatting | bytes 4194304
  313.0 9.8 %copy.94 = f32[2,16,8,16,128]{4,3,2,1,0:T(8,128)S(1)} copy(f32[2,16,8,16,128]{3,1,0,4,2:T(8,128)} %bitcast.284) | data formatting | bytes 4194304 | tf_op jit(solution)/shard_map/all_to_all | solution.py:53
  322.8 57.8 %bitcast_divide_fusion.1 = f32[2,2048,128]{2,1,0:T(8,128)S(1)} fusion(f32[2,16,8,16,128]{4,3,2,1,0:T(8,128)S(1)} %copy.94, f32[2,2048,128]{2,1,0:T(8,128)} %bitcast.291, f32[]{:T(128)} %bitcast.88, f32[]{:T(128)} %bitcast.87, f32[]{:T(128)} %bitcast.86, f32[]{:T(128)} %bitcast.85, f32[]{:T(128)} %bitcast.84, f32[]{:T(128)} %bitcast.83, f32[]{:T(128)} %bitcast.82, ...), kind=kLoop, calls=%fused_computation.373 | loop fusion | flops 33030144 | bytes 6291580 | tf_op jit(solution)/shard_map/div | solution.py:96
  380.6 27.4 %multiply_add_fusion.1 = f32[2,2048,128]{2,1,0:T(8,128)S(1)} fusion(f32[2,2048,128]{2,1,0:T(8,128)S(1)} %bitcast_divide_fusion.1, f32[]{:T(128)} %bitcast.118, f32[]{:T(128)} %bitcast.117, f32[]{:T(128)} %bitcast.116, f32[]{:T(128)} %bitcast.115, f32[]{:T(128)} %bitcast.114, f32[]{:T(128)} %bitcast.113, f32[]{:T(128)} %bitcast.112, f32[]{:T(128)} %bitcast.111, ...), kind=kLoop, calls=%fused_computation.430 | loop fusion | flops 31981568 | bytes 4194428 | tf_op jit(solution)/shard_map/add | solution.py:32
  408.3 34.8 %all_to_all.190 = f32[2,16,128,128]{3,2,0,1:T(8,128)S(1)} all-to-all(f32[2,16,128,128]{3,2,0,1:T(8,128)S(1)} %copy.100), channel_id=1, replica_groups=mesh['scan'=16,'row'=8] {'scan'}, dimensions={1} | all-to-all | bytes 4194304 | tf_op jit(solution)/shard_map/all_to_all | solution.py:65
  452.8 25.0 %all-to-all-done.6 = f32[32,1,128,128]{3,0,1,2:T(8,128)} async-done(((f32[32,1,128,128]{3,0,1,2:T(8,128)}), f32[32,1,128,128]{3,0,1,2:T(8,128)}, u32[]{:S(2)}, u32[]{:S(2)}) %all-to-all-start.6) | async-done | bytes 2097184 | tf_op jit(solution)/shard_map/all_to_all | solution.py:64
  482.0 36.3 %fusion.113 = f32[32,1,16,1024]{3,2,1,0:T(8,128)S(1)} fusion(f32[32,1,16,1024]{3,2,1,0:T(8,128)S(1)} %copy.104, f32[]{:T(128)} %bitcast.155, f32[]{:T(128)} %bitcast.154, f32[]{:T(128)} %bitcast.153, f32[]{:T(128)} %bitcast.152, f32[]{:T(128)} %bitcast.151, f32[]{:T(128)} %bitcast.150, f32[]{:T(128)} %bitcast.149, f32[]{:T(128)} %bitcast.148, f32[]{:T(128)} %bitcast.147, ...), kind=kLoop, calls=%fused_computation.239 | loop fusion | flops 31981568 | bytes 4194428 | tf_op jit(solution)/shard_map/add | solution.py:32
  526.9 36.0 %fusion.173 = f32[32,1,16,1024]{3,2,1,0:T(8,128)S(1)} fusion(f32[32,1,16,1024]{3,2,1,0:T(8,128)S(1)} %bitcast.297, f32[]{:T(128)} %bitcast.50, f32[]{:T(128)} %bitcast.49, f32[]{:T(128)} %bitcast.48, f32[]{:T(128)} %bitcast.47, f32[]{:T(128)} %bitcast.46, f32[]{:T(128)} %bitcast.45, f32[]{:T(128)} %bitcast.44, f32[]{:T(128)} %bitcast.43, f32[]{:T(128)} %bitcast.42, ...), kind=kLoop, calls=%fused_computation.299 | loop fusion | flops 31981568 | bytes 4194428 | tf_op jit(solution)/shard_map/add | solution.py:32
  562.9 30.6 %all_to_all.191 = f32[32,1,16,1024]{3,2,1,0:T(8,128)} all-to-all(f32[32,1,16,1024]{3,2,1,0:T(8,128)S(1)} %fusion.173), channel_id=1, replica_groups=mesh['scan'=16,'row'=8] {'scan'}, dimensions={0} | all-to-all | bytes 4194304 | tf_op jit(solution)/shard_map/all_to_all | solution.py:54
  593.5 21.4 %copy.111 = f32[2,16,16,1024]{2,0,1,3:T(2,128)} copy(f32[2,16,16,1024]{3,2,0,1:T(8,128)} %bitcast.294) | data formatting | bytes 4194304 | tf_op jit(solution)/shard_map/all_to_all | solution.py:54
  614.9 24.7 %reshape.190 = f32[8,1,65536]{2,1,0:T(1,128)} reshape(f32[1024,16,2,16]{3,2,1,0:T(2,128)} %bitcast.285) | data formatting | bytes 4194304
  639.7 32.8 %all_to_all.192 = f32[8,1,65536]{2,1,0:T(1,128)} all-to-all(f32[8,1,65536]{2,1,0:T(1,128)} %reshape.190), channel_id=1, replica_groups=mesh['scan'=16,'row'=8] {'row'}, dimensions={0} | all-to-all | bytes 4194304 | tf_op jit(solution)/shard_map/all_to_all | solution.py:53
  672.5 8.6 reduce.4
  681.1 31.8 %reshape.191 = f32[1024,16,2,16]{3,2,1,0:T(2,128)} reshape(f32[8,65536]{1,0:T(8,128)} %reduce.4) | data formatting | bytes 4194304
  712.9 21.6 %copy.133 = f32[2,16,16,8,128]{4,2,3,1,0:T(8,128)} copy(f32[2,16,16,8,128]{2,0,1,4,3:T(2,128)} %bitcast.286) | data formatting | bytes 4194304 | tf_op jit(solution)/shard_map/all_to_all | solution.py:53
  734.5 57.3 %bitcast_divide_fusion = f32[2,2048,128]{2,1,0:T(8,128)S(1)} fusion(f32[2,16,8,16,128]{4,3,2,1,0:T(8,128)S(1)} %copy.94, f32[2,2048,128]{2,1,0:T(8,128)} %bitcast.290, f32[]{:T(128)} %bitcast.88, f32[]{:T(128)} %bitcast.87, f32[]{:T(128)} %bitcast.86, f32[]{:T(128)} %bitcast.85, f32[]{:T(128)} %bitcast.84, f32[]{:T(128)} %bitcast.83, f32[]{:T(128)} %bitcast.82, ...), kind=kLoop, calls=%fused_computation.372 | loop fusion | flops 33030144 | bytes 6291580 | tf_op jit(solution)/shard_map/div | solution.py:96
  791.8 27.6 %multiply_add_fusion = f32[2,2048,128]{2,1,0:T(8,128)S(1)} fusion(f32[2,2048,128]{2,1,0:T(8,128)S(1)} %bitcast_divide_fusion, f32[]{:T(128)} %bitcast.118, f32[]{:T(128)} %bitcast.117, f32[]{:T(128)} %bitcast.116, f32[]{:T(128)} %bitcast.115, f32[]{:T(128)} %bitcast.114, f32[]{:T(128)} %bitcast.113, f32[]{:T(128)} %bitcast.112, f32[]{:T(128)} %bitcast.111, ...), kind=kLoop, calls=%fused_computation.377 | loop fusion | flops 31981568 | bytes 4194428 | tf_op jit(solution)/shard_map/add | solution.py:32
  819.6 29.8 %all_to_all.193 = f32[2,16,128,128]{3,2,0,1:T(8,128)S(1)} all-to-all(f32[2,16,128,128]{3,2,0,1:T(8,128)S(1)} %copy.114), channel_id=1, replica_groups=mesh['scan'=16,'row'=8] {'scan'}, dimensions={1} | all-to-all | bytes 4194304 | tf_op jit(solution)/shard_map/all_to_all | solution.py:65
  850.7 31.1 %all_to_all.194 = f32[32,1,128,128]{3,0,1,2:T(8,128)S(1)} all-to-all(f32[32,1,128,128]{3,0,1,2:T(8,128)S(1)} %copy.115), channel_id=1, replica_groups=mesh['scan'=16,'row'=8] {'row'}, dimensions={2} | all-to-all | bytes 4194304 | tf_op jit(solution)/shard_map/all_to_all | solution.py:64
  884.4 36.1 %fusion.233 = f32[32,1,16,1024]{3,2,1,0:T(8,128)S(1)} fusion(f32[32,1,16,1024]{3,2,1,0:T(8,128)S(1)} %copy.118, f32[]{:T(128)} %bitcast.155, f32[]{:T(128)} %bitcast.154, f32[]{:T(128)} %bitcast.153, f32[]{:T(128)} %bitcast.152, f32[]{:T(128)} %bitcast.151, f32[]{:T(128)} %bitcast.150, f32[]{:T(128)} %bitcast.149, f32[]{:T(128)} %bitcast.148, f32[]{:T(128)} %bitcast.147, ...), kind=kLoop, calls=%fused_computation.359 | loop fusion | flops 31981568 | bytes 4194428 | tf_op jit(solution)/shard_map/add | solution.py:32
  (85 shorter events, 104.8 us)
Async XLA Ops:
  0.0 3.2 copy-start.5
  0.0 3.2 copy-start.4
  20.8 8.8 copy-start.6
  20.8 9.6 %copy-start.8 = (f32[64]{0:T(128)S(1)}, f32[64]{0:T(128)}, u32[]{:S(2)}) copy-start(f32[64]{0:T(128)} %param.7) | copy-start | bytes 772
  20.8 39.3 %all-to-all-start = ((f32[2,16,16,1024]{3,2,0,1:T(8,128)}), f32[2,16,16,1024]{3,2,0,1:T(8,128)}, u32[]{:S(2)}, u32[]{:S(2)}) async-start(f32[2,16,16,1024]{3,2,0,1:T(8,128)} %get-tuple-element.10), calls=%async_computation | async-start | bytes 4194304 | tf_op jit(solution)/shard_map/all_to_all | solution.py:84
  61.9 1.3 copy-start.2
  133.6 50.2 %all-to-all-start.1 = ((f32[32,1,16,1024]{3,2,1,0:T(8,128)}), f32[32,1,16,1024]{3,2,1,0:T(8,128)S(1)}, u32[]{:S(2)}, u32[]{:S(2)}) async-start(f32[32,1,16,1024]{3,2,1,0:T(8,128)} %bitcast.9), calls=%async_computation.1 | async-start | bytes 4194304 | tf_op jit(solution)/shard_map/all_to_all | solution.py:54
  183.9 43.3 %all-to-all-start.4 = ((f32[8,1,65536]{2,1,0:T(1,128)}), f32[8,1,65536]{2,1,0:T(1,128)}, u32[]{:S(2)}, u32[]{:S(2)}) async-start(f32[8,1,65536]{2,1,0:T(1,128)} %reshape.188), calls=%async_computation.4 | async-start | bytes 4194304 | tf_op jit(solution)/shard_map/all_to_all | solution.py:53
  227.2 4.9 copy-start.7
  227.2 67.3 %all-to-all-start.2 = ((f32[8,1,65536]{2,1,0:T(1,128)}), f32[8,1,65536]{2,1,0:T(1,128)}, u32[]{:S(2)}, u32[]{:S(2)}) async-start(f32[8,1,65536]{2,1,0:T(1,128)} %reshape.186), calls=%async_computation.2 | async-start | bytes 4194304 | tf_op jit(solution)/shard_map/all_to_all | solution.py:53
  445.6 32.2 %all-to-all-start.6 = ((f32[32,1,128,128]{3,0,1,2:T(8,128)}), f32[32,1,128,128]{3,0,1,2:T(8,128)}, u32[]{:S(2)}, u32[]{:S(2)}) async-start(f32[32,1,128,128]{3,0,1,2:T(8,128)} %copy.101), calls=%async_computation.6 | async-start | bytes 4194304 | tf_op jit(solution)/shard_map/all_to_all | solution.py:64
  482.0 36.3 %copy-start.3 = (f32[16,2,1,16,1024]{4,3,1,0,2:T(8,128)S(1)}, f32[16,2,1,16,1024]{4,3,1,0,2:T(8,128)}, u32[]{:S(2)}) copy-start(f32[16,2,1,16,1024]{4,3,1,0,2:T(8,128)} %copy-done.2) | copy-start | bytes 6291460
  522.5 1.3 copy-start
  884.4 36.2 %copy-start.1 = (f32[32,16,1024]{2,0,1:T(8,128)S(1)}, f32[32,16,1024]{2,0,1:T(8,128)}, u32[]{:S(2)}) copy-start(f32[32,16,1024]{2,0,1:T(8,128)} %copy-done) | copy-start | bytes 6291460
where the time goes:
time: 942 us; the launch traced here: 927 us
  other arithmetic  357 us (38%)
  local copies, waits for them, and re-layouts  293 us (31%)
  blocking collectives  190 us (20%)
  waiting for transfers between devices  44.7 us (5%)
  starting transfers between devices  30.1 us (3%)
  matrix products  11 us (1%)
    add x6, other arithmetic, shifted_sum(): summed + kernel[tap] * lax.slice_in_dim(padded, tap, tap + extent, axis=a...  199 us
    unnamed x30, local copies, waits for them, and re-layouts  149 us
    div x2, other arithmetic, shards(): quotient = data_flat / (flattened + background_level)  115 us
    all_to_all x2, blocking collectives, pencil_layout(): lax.all_to_all(volume, 'scan', split_axis=1, concat_axis=0, tiled=True)  64.6 us
    all_to_all x2, blocking collectives, rows_layout(): lax.all_to_all(volume, 'scan', split_axis=0, concat_axis=1, tiled=True)  61.9 us
    all_to_all x3, local copies, waits for them, and re-layouts, rows_layout(): lax.all_to_all(volume, 'scan', split_axis=0, concat_axis=1, tiled=True)  56.4 us
    all_to_all x4, local copies, waits for them, and re-layouts, rows_layout(): lax.all_to_all(lax.all_to_all(volume, 'scan', split_axis=0, concat_axis=1...  53.8 us
    all_to_all x1, blocking collectives, rows_layout(): lax.all_to_all(lax.all_to_all(volume, 'scan', split_axis=0, concat_axis=1...  32.8 us
  transfers between devices with their start and end apart: 5, of which 2 were waited for; matrix products, arithmetic and copies ran while one was open for 17% of the time, Pallas kernels for 0%

commit v1 on v0

--- a/solution.py
+++ b/solution.py
@@ -50,13 +50,11 @@
 
 
 def rows_layout(volume):
-    result = lax.all_to_all(
-        lax.all_to_all(volume, "scan", split_axis=0, concat_axis=1, tiled=True),
-        "row",
-        split_axis=3,
-        concat_axis=2,
-        tiled=True,
-    )
+    own = lax.all_to_all(volume, "scan", split_axis=0, concat_axis=1, tiled=True)
+    size = lax.axis_size("row")
+    parts = jnp.stack(jnp.split(own, size, axis=3), axis=0)
+    parts = lax.all_to_all(parts, "row", split_axis=0, concat_axis=0)
+    result = jnp.concatenate(parts, axis=2)
     return result
 
 

time: 942 us -> 682 us (0.72)
  local copies, waits for them, and re-layouts: 293 us -> 60.7 us
  other arithmetic: 357 us -> 281 us
  waiting for transfers between devices: 44.7 us -> 101 us
    unnamed x30 -> x46, local copies, waits for them, and re-layouts: 149 us -> 20 us
    all_to_all x7 -> x0, local copies, waits for them, and re-layouts: 110 us -> none  [the longest x3 56.4 us: rows_layout(): lax.all_to_all(volume, 'scan', split_axis=0, concat_axis=1, tiled=True)]
    div x2, other arithmetic: 115 us -> 55.3 us  [shards(): quotient = data_flat / (flattened + background_level)]
    all_to_all x2, waiting for transfers between devices: 0.01 us -> 39.3 us  [rows_layout(): parts = lax.all_to_all(parts, 'row', split_axis=0, concat_axis=0)]
    all_to_all x3 -> x0, other arithmetic: 23.1 us -> none  [rows_layout(): lax.all_to_all(lax.all_to_all(volume, 'scan', split_axis=0, concat_axis=1...]
    all_to_all x1, waiting for transfers between devices: 0.01 us -> 16.4 us  [rows_layout(): lax.all_to_all(volume, 'scan', split_axis=0, concat_axis=1, tiled=True)]
  transfers between devices with their start and end apart: 5 -> 5, of which waited for: 2 -> 5; matrix products, arithmetic and copies ran while one was open for 17% -> 5% of each run, Pallas kernels for 0% -> 0%
where the time goes in v1:
time: 682 us; the launch traced here: 671 us
  other arithmetic  281 us (41%)
  blocking collectives  184 us (27%)
  waiting for transfers between devices  101 us (15%)
  local copies, waits for them, and re-layouts  60.7 us (9%)
  starting transfers between devices  32.7 us (5%)
  matrix products  11 us (2%)
    add x6, other arithmetic, shifted_sum(): summed + kernel[tap] * lax.slice_in_dim(padded, tap, tap + extent, axis=a...  207 us
    all_to_all x2, blocking collectives, rows_layout(): lax.all_to_all(volume, 'scan', split_axis=0, concat_axis=1, tiled=True)  61.2 us
    all_to_all x2, blocking collectives, pencil_layout(): lax.all_to_all(volume, 'scan', split_axis=1, concat_axis=0, tiled=True)  59.8 us
    div x2, other arithmetic, shards(): quotient = data_flat / (flattened + background_level)  55.3 us
    all_to_all x2, waiting for transfers between devices, rows_layout(): parts = lax.all_to_all(parts, 'row', split_axis=0, concat_axis=0)  39.3 us
    all_to_all x1, blocking collectives, pencil_layout(): lax.all_to_all(lax.all_to_all(volume, 'scan', split_axis=1, concat_axis=0...  31.4 us
    all_to_all x1, blocking collectives, rows_layout(): parts = lax.all_to_all(parts, 'row', split_axis=0, concat_axis=0)  31.2 us
    all_to_all x1, waiting for transfers between devices, pencil_layout(): lax.all_to_all(lax.all_to_all(volume, 'scan', split_axis=1, concat_axis=0...  25 us
  transfers between devices with their start and end apart: 5, of which 5 were waited for; matrix products, arithmetic and copies ran while one was open for 5% of the time, Pallas kernels for 0%

profile of v1, /device:TPU:1, one launch (start us, length us, event | category | flops | bytes accessed | tf_op | source)
XLA Modules:
  0.0 670.6 jit_solution(1431313124974799359)
XLA Ops:
  3.2 17.9 %while.1 = (s32[]{:T(128)}, f32[2,16,16,1024]{3,2,0,1:T(8,128)}, s32[2,4]{1,0:T(2,128)S(1)}, f32[2,6,16,1024]{3,2,1,0:T(8,128)S(1)}, s32[]{:T(128)}, /*index=5*/s32[4]{0:T(128)S(1)}) while((s32[]{:T(128)}, f32[2,16,16,1024]{3,2,0,1:T(8,128)}, s32[2,4]{1,0:T(2,128)S(1)}, f32[2,6,16,1024]{3,2,1,0:T(8,128)S(1)}, s32[]{:T(128)}, ...), condition=%wide.while_cond, body=%wide.while_body.sunk | while | flops 98333 | bytes 1968306 | solution.py:41
  3.8 3.3 and_reduce_fusion.2
  12.8 3.3 and_reduce_fusion.2
  21.1 8.8 %all-to-all-start = ((f32[2,16,16,1024]{3,2,0,1:T(8,128)}), f32[2,16,16,1024]{3,2,0,1:T(8,128)}, u32[]{:S(2)}, u32[]{:S(2)}) async-start(f32[2,16,16,1024]{3,2,0,1:T(8,128)} %get-tuple-element.10), calls=%async_computation | async-start | bytes 4194304 | tf_op jit(solution)/shard_map/all_to_all | solution.py:82
  31.9 6.6 gather_fusion
  40.6 19.8 %all-to-all-done = f32[2,16,16,1024]{3,2,0,1:T(8,128)} async-done(((f32[2,16,16,1024]{3,2,0,1:T(8,128)}), f32[2,16,16,1024]{3,2,0,1:T(8,128)}, u32[]{:S(2)}, u32[]{:S(2)}) %all-to-all-start) | async-done | bytes 2097184 | tf_op jit(solution)/shard_map/all_to_all | solution.py:82
  66.8 35.8 %fusion.53 = f32[32,1,16,1024]{3,2,1,0:T(8,128)S(1)} fusion(f32[32,1,16,1024]{3,2,1,0:T(8,128)S(1)} %bitcast.396, f32[]{:T(128)} %bitcast.58, f32[]{:T(128)} %bitcast.57, f32[]{:T(128)} %bitcast.56, f32[]{:T(128)} %bitcast.55, f32[]{:T(128)} %bitcast.54, f32[]{:T(128)} %bitcast.53, f32[]{:T(128)} %bitcast.52, f32[]{:T(128)} %bitcast.51, f32[]{:T(128)} %bitcast.50, ...), kind=kLoop, calls=%fused_computation.179 | loop fusion | flops 31981568 | bytes 4194428 | tf_op jit(solution)/shard_map/add | solution.py:32
  102.6 31.3 %all_to_all.159 = f32[32,1,16,1024]{3,2,1,0:T(8,128)} all-to-all(f32[32,1,16,1024]{3,2,1,0:T(8,128)S(1)} %fusion.53), channel_id=1, replica_groups=mesh['scan'=16,'row'=8] {'scan'}, dimensions={0} | all-to-all | bytes 4194304 | tf_op jit(solution)/shard_map/all_to_all | solution.py:53
  133.8 3.7 all-to-all-start.1
  147.4 16.4 %all-to-all-done.1 = f32[32,1,16,1024]{3,2,1,0:T(8,128)S(1)} async-done(((f32[32,1,16,1024]{3,2,1,0:T(8,128)}), f32[32,1,16,1024]{3,2,1,0:T(8,128)S(1)}, u32[]{:S(2)}, u32[]{:S(2)}) %all-to-all-start.1) | async-done | bytes 2097184 | tf_op jit(solution)/shard_map/all_to_all | solution.py:53
  163.9 9.4 %all-to-all-start.4 = ((f32[8,2,16,16,128]{4,3,1,2,0:T(8,128)}), f32[8,2,16,16,128]{4,3,1,2,0:T(8,128)}, u32[]{:S(2)}, u32[]{:S(2)}) async-start(f32[8,2,16,16,128]{4,3,1,2,0:T(8,128)} %fusion.326), calls=%async_computation.4 | async-start | bytes 4194304 | tf_op jit(solution)/shard_map/all_to_all | solution.py:56
  179.3 20.4 %all-to-all-done.4 = f32[8,2,16,16,128]{4,3,1,2,0:T(8,128)} async-done(((f32[8,2,16,16,128]{4,3,1,2,0:T(8,128)}), f32[8,2,16,16,128]{4,3,1,2,0:T(8,128)}, u32[]{:S(2)}, u32[]{:S(2)}) %all-to-all-start.4) | async-done | bytes 2097184 | tf_op jit(solution)/shard_map/all_to_all | solution.py:56
  199.7 4.7 all-to-all-start.2
  208.6 3.2 copy.89
  211.8 18.9 %all-to-all-done.2 = f32[8,2,16,16,128]{4,3,1,2,0:T(8,128)S(1)} async-done(((f32[8,2,16,16,128]{4,3,1,2,0:T(8,128)}), f32[8,2,16,16,128]{4,3,1,2,0:T(8,128)S(1)}, u32[]{:S(2)}, u32[]{:S(2)}) %all-to-all-start.2) | async-done | bytes 2097184 | tf_op jit(solution)/shard_map/all_to_all | solution.py:56
  234.2 27.6 %bitcast_divide_fusion.1 = f32[2,2048,128]{2,1,0:T(8,128)S(1)} fusion(f32[2,16,8,16,128]{4,3,2,1,0:T(8,128)S(1)} %copy.86, f32[2,2048,128]{2,1,0:T(8,128)S(1)} %bitcast.390, f32[]{:T(128)} %bitcast.103, f32[]{:T(128)} %bitcast.102, f32[]{:T(128)} %bitcast.101, f32[]{:T(128)} %bitcast.100, f32[]{:T(128)} %bitcast.99, f32[]{:T(128)} %bitcast.98, f32[]{:T(128)} %bitcast.97, ...), kind=kLoop, calls=%fused_computation.373 | loop fusion | flops 33030144 | bytes 6291580 | tf_op jit(solution)/shard_map/div | solution.py:94
  261.8 27.3 %multiply_add_fusion.1 = f32[2,2048,128]{2,1,0:T(8,128)S(1)} fusion(f32[2,2048,128]{2,1,0:T(8,128)S(1)} %bitcast_divide_fusion.1, f32[]{:T(128)} %bitcast.133, f32[]{:T(128)} %bitcast.132, f32[]{:T(128)} %bitcast.131, f32[]{:T(128)} %bitcast.130, f32[]{:T(128)} %bitcast.129, f32[]{:T(128)} %bitcast.128, f32[]{:T(128)} %bitcast.127, f32[]{:T(128)} %bitcast.126, ...), kind=kLoop, calls=%fused_computation.430 | loop fusion | flops 31981568 | bytes 4194428 | tf_op jit(solution)/shard_map/add | solution.py:32
  289.4 30.0 %all_to_all.160 = f32[2,16,128,128]{3,2,0,1:T(8,128)S(1)} all-to-all(f32[2,16,128,128]{3,2,0,1:T(8,128)S(1)} %copy.90), channel_id=1, replica_groups=mesh['scan'=16,'row'=8] {'scan'}, dimensions={1} | all-to-all | bytes 4194304 | tf_op jit(solution)/shard_map/all_to_all | solution.py:63
  322.0 6.2 all-to-all-start.6
  329.6 25.0 %all-to-all-done.6 = f32[32,1,128,128]{3,0,1,2:T(8,128)} async-done(((f32[32,1,128,128]{3,0,1,2:T(8,128)}), f32[32,1,128,128]{3,0,1,2:T(8,128)}, u32[]{:S(2)}, u32[]{:S(2)}) %all-to-all-start.6) | async-done | bytes 2097184 | tf_op jit(solution)/shard_map/all_to_all | solution.py:62
  354.6 2.8 copy.92
  358.8 44.8 %fusion.113 = f32[32,1,16,1024]{3,2,1,0:T(8,128)S(1)} fusion(f32[32,1,16,1024]{3,2,1,0:T(8,128)S(1)} %copy.94, f32[]{:T(128)} %bitcast.170, f32[]{:T(128)} %bitcast.169, f32[]{:T(128)} %bitcast.168, f32[]{:T(128)} %bitcast.167, f32[]{:T(128)} %bitcast.166, f32[]{:T(128)} %bitcast.165, f32[]{:T(128)} %bitcast.164, f32[]{:T(128)} %bitcast.163, f32[]{:T(128)} %bitcast.162, ...), kind=kLoop, calls=%fused_computation.239 | loop fusion | flops 31981568 | bytes 4194428 | tf_op jit(solution)/shard_map/add | solution.py:32
  403.6 4.1 copy_multiply_fusion
  411.1 35.8 %fusion.173 = f32[32,1,16,1024]{3,2,1,0:T(8,128)S(1)} fusion(f32[32,1,16,1024]{3,2,1,0:T(8,128)S(1)} %bitcast.394, f32[]{:T(128)} %bitcast.58, f32[]{:T(128)} %bitcast.57, f32[]{:T(128)} %bitcast.56, f32[]{:T(128)} %bitcast.55, f32[]{:T(128)} %bitcast.54, f32[]{:T(128)} %bitcast.53, f32[]{:T(128)} %bitcast.52, f32[]{:T(128)} %bitcast.51, f32[]{:T(128)} %bitcast.50, ...), kind=kLoop, calls=%fused_computation.299 | loop fusion | flops 31981568 | bytes 4194428 | tf_op jit(solution)/shard_map/add | solution.py:32
  446.9 30.0 %all_to_all.161 = f32[32,1,16,1024]{3,2,1,0:T(8,128)S(1)} all-to-all(f32[32,1,16,1024]{3,2,1,0:T(8,128)S(1)} %fusion.173), channel_id=1, replica_groups=mesh['scan'=16,'row'=8] {'scan'}, dimensions={0} | all-to-all | bytes 4194304 | tf_op jit(solution)/shard_map/all_to_all | solution.py:53
  477.2 31.2 %all_to_all.162 = f32[8,2,16,16,128]{4,3,1,2,0:T(8,128)S(1)} all-to-all(f32[8,2,16,16,128]{4,3,1,2,0:T(8,128)S(1)} %fusion.318), channel_id=1, replica_groups=mesh['scan'=16,'row'=8] {'row'}, dimensions={0} | all-to-all | bytes 4194304 | tf_op jit(solution)/shard_map/all_to_all | solution.py:56
  508.6 27.6 %bitcast_divide_fusion = f32[2,2048,128]{2,1,0:T(8,128)S(1)} fusion(f32[2,16,8,16,128]{4,3,2,1,0:T(8,128)S(1)} %copy.86, f32[2,2048,128]{2,1,0:T(8,128)S(1)} %bitcast.373, f32[]{:T(128)} %bitcast.103, f32[]{:T(128)} %bitcast.102, f32[]{:T(128)} %bitcast.101, f32[]{:T(128)} %bitcast.100, f32[]{:T(128)} %bitcast.99, f32[]{:T(128)} %bitcast.98, f32[]{:T(128)} %bitcast.97, ...), kind=kLoop, calls=%fused_computation.372 | loop fusion | flops 33030144 | bytes 6291580 | tf_op jit(solution)/shard_map/div | solution.py:94
  536.2 27.3 %multiply_add_fusion = f32[2,2048,128]{2,1,0:T(8,128)S(1)} fusion(f32[2,2048,128]{2,1,0:T(8,128)S(1)} %bitcast_divide_fusion, f32[]{:T(128)} %bitcast.133, f32[]{:T(128)} %bitcast.132, f32[]{:T(128)} %bitcast.131, f32[]{:T(128)} %bitcast.130, f32[]{:T(128)} %bitcast.129, f32[]{:T(128)} %bitcast.128, f32[]{:T(128)} %bitcast.127, f32[]{:T(128)} %bitcast.126, ...), kind=kLoop, calls=%fused_computation.377 | loop fusion | flops 31981568 | bytes 4194428 | tf_op jit(solution)/shard_map/add | solution.py:32
  563.7 29.8 %all_to_all.163 = f32[2,16,128,128]{3,2,0,1:T(8,128)S(1)} all-to-all(f32[2,16,128,128]{3,2,0,1:T(8,128)S(1)} %copy.102), channel_id=1, replica_groups=mesh['scan'=16,'row'=8] {'scan'}, dimensions={1} | all-to-all | bytes 4194304 | tf_op jit(solution)/shard_map/all_to_all | solution.py:63
  594.7 31.4 %all_to_all.164 = f32[32,1,128,128]{3,0,1,2:T(8,128)S(1)} all-to-all(f32[32,1,128,128]{3,0,1,2:T(8,128)S(1)} %copy.103), channel_id=1, replica_groups=mesh['scan'=16,'row'=8] {'row'}, dimensions={2} | all-to-all | bytes 4194304 | tf_op jit(solution)/shard_map/all_to_all | solution.py:62
  628.7 35.9 %fusion.233 = f32[32,1,16,1024]{3,2,1,0:T(8,128)S(1)} fusion(f32[32,1,16,1024]{3,2,1,0:T(8,128)S(1)} %copy.106, f32[]{:T(128)} %bitcast.170, f32[]{:T(128)} %bitcast.169, f32[]{:T(128)} %bitcast.168, f32[]{:T(128)} %bitcast.167, f32[]{:T(128)} %bitcast.166, f32[]{:T(128)} %bitcast.165, f32[]{:T(128)} %bitcast.164, f32[]{:T(128)} %bitcast.163, f32[]{:T(128)} %bitcast.162, ...), kind=kLoop, calls=%fused_computation.359 | loop fusion | flops 31981568 | bytes 4194428 | tf_op jit(solution)/shard_map/add | solution.py:32
  664.6 3.1 multiply_bitcast_fusion
  (97 shorter events, 64.4 us)
Async XLA Ops:
  0.0 3.2 copy-start.6
  0.0 3.2 copy-start.5
  21.1 8.8 %copy-start.7 = (f32[31]{0:T(128)S(1)}, f32[31]{0:T(128)}, u32[]{:S(2)}) copy-start(f32[31]{0:T(128)} %param.8) | copy-start | bytes 376
  21.1 9.6 %copy-start.9 = (f32[64]{0:T(128)S(1)}, f32[64]{0:T(128)}, u32[]{:S(2)}) copy-start(f32[64]{0:T(128)} %param.7) | copy-start | bytes 772
  21.1 39.3 %all-to-all-start = ((f32[2,16,16,1024]{3,2,0,1:T(8,128)}), f32[2,16,16,1024]{3,2,0,1:T(8,128)}, u32[]{:S(2)}, u32[]{:S(2)}) async-start(f32[2,16,16,1024]{3,2,0,1:T(8,128)} %get-tuple-element.10), calls=%async_computation | async-start | bytes 4194304 | tf_op jit(solution)/shard_map/all_to_all | solution.py:82
  62.3 1.3 copy-start
  133.8 30.0 %all-to-all-start.1 = ((f32[32,1,16,1024]{3,2,1,0:T(8,128)}), f32[32,1,16,1024]{3,2,1,0:T(8,128)S(1)}, u32[]{:S(2)}, u32[]{:S(2)}) async-start(f32[32,1,16,1024]{3,2,1,0:T(8,128)} %bitcast.9), calls=%async_computation.1 | async-start | bytes 4194304 | tf_op jit(solution)/shard_map/all_to_all | solution.py:53
  137.6 6.9 %copy-start.2 = (f32[32,1,16,1024]{3,2,1,0:T(8,128)S(1)}, f32[32,1,16,1024]{3,2,1,0:T(8,128)}, u32[]{:S(2)}) copy-start(f32[32,1,16,1024]{3,2,1,0:T(8,128)} %all_to_all.159) | copy-start | bytes 6291460
  163.9 35.8 %all-to-all-start.4 = ((f32[8,2,16,16,128]{4,3,1,2,0:T(8,128)}), f32[8,2,16,16,128]{4,3,1,2,0:T(8,128)}, u32[]{:S(2)}, u32[]{:S(2)}) async-start(f32[8,2,16,16,128]{4,3,1,2,0:T(8,128)} %fusion.326), calls=%async_computation.4 | async-start | bytes 4194304 | tf_op jit(solution)/shard_map/all_to_all | solution.py:56
  179.3 25.1 %copy-start.8 = (f32[31]{0:T(128)S(1)}, f32[31]{0:T(128)}, u32[]{:S(2)}) copy-start(f32[31]{0:T(128)} %param.9) | copy-start | bytes 376
  199.7 31.0 %all-to-all-start.2 = ((f32[8,2,16,16,128]{4,3,1,2,0:T(8,128)}), f32[8,2,16,16,128]{4,3,1,2,0:T(8,128)S(1)}, u32[]{:S(2)}, u32[]{:S(2)}) async-start(f32[8,2,16,16,128]{4,3,1,2,0:T(8,128)} %fusion.334), calls=%async_computation.2 | async-start | bytes 4194304 | tf_op jit(solution)/shard_map/all_to_all | solution.py:56
  230.7 1.3 copy-start.4
  232.0 2.2 copy-start.3
  322.0 32.7 %all-to-all-start.6 = ((f32[32,1,128,128]{3,0,1,2:T(8,128)}), f32[32,1,128,128]{3,0,1,2:T(8,128)}, u32[]{:S(2)}, u32[]{:S(2)}) async-start(f32[32,1,128,128]{3,0,1,2:T(8,128)} %copy.91), calls=%async_computation.6 | async-start | bytes 4194304 | tf_op jit(solution)/shard_map/all_to_all | solution.py:62
  358.8 44.8 %copy-start.1 = (f32[16,2,1,16,1024]{4,3,1,0,2:T(8,128)S(1)}, f32[16,2,1,16,1024]{4,3,1,0,2:T(8,128)}, u32[]{:S(2)}) copy-start(f32[16,2,1,16,1024]{4,3,1,0,2:T(8,128)} %copy-done) | copy-start | bytes 6291460
